TPU v7x, 32 devices: a whole 2x2x4 slice. The times are simulated.
32 devices in a mesh: dp: 2 (over x), tok: 4 (over z), mp: 4 (over y, core).
Axes of the slice: x: 2, y: 2, z: 4, core: 2. Of those that a mesh axis runs over, the one named last changes fastest.
Arguments:
- tokens: bfloat16 [16384, 1024], P(('dp', 'tok'), 'mp'), may hold values from -6 to 6
- in_weight: bfloat16 [1024, 3, 1024], P(('dp', 'tok'), None, 'mp'), may hold values from -0.1875 to 0.1875
- conv_kernel: bfloat16 [3, 1024], P(None, 'mp'), may hold values from -2.5 to 2.5
- out_weight: bfloat16 [1024, 1024], P('mp', ('dp', 'tok')), may hold values from -0.1875 to 0.1875
- gate_weight: bfloat16 [1024, 4608], P(('dp', 'tok'), 'mp'), may hold values from -0.1875 to 0.1875
- up_weight: bfloat16 [1024, 4608], P(('dp', 'tok'), 'mp'), may hold values from -0.1875 to 0.1875
- down_weight: bfloat16 [4608, 1024], P('mp', ('dp', 'tok')), may hold values from -0.09375 to 0.09375
- mixer_norm_gain: float32 [1024], replicated, may hold values from 0.5 to 1.5
- gain_ffn: float32 [1024], replicated, may hold values from 0.5 to 1.5
- cotangent: bfloat16 [16384, 1024], P(('dp', 'tok'), 'mp'), may hold values from -6 to 6
Outputs:
- mixed: bfloat16 [16384, 1024], P(('dp', 'tok'), 'mp')
- input_token_gradient: float32 [16384, 1024], P(('dp', 'tok'), 'mp')
- grad_in_weight: float32 [1024, 3, 1024], P(('dp', 'tok'), None, 'mp')
- grad_conv_kernel: float32 [3, 1024], P(None, 'mp')
- grad_out_weight: float32 [1024, 1024], P('mp', ('dp', 'tok'))
- grad_gate_weight: float32 [1024, 4608], P(('dp', 'tok'), 'mp')
- grad_up_weight: float32 [1024, 4608], P(('dp', 'tok'), 'mp')
- grad_down_weight: float32 [4608, 1024], P('mp', ('dp', 'tok'))
- grad_gain_mix: float32 [1024], P('mp')
- grad_gain_ffn: float32 [1024], P('mp')
All inputs are finite; a program needn't handle non-finite values.
Results may differ from a plain program's by a relative error of at most 0.011.
Values may be sent and summed in bfloat16 or wider, within the bound.
No kernel may reach another device: no remote copies, remote signals or barrier semaphores. Data moves between devices by JAX's collectives and lax.ppermute only.
A program may use at most 192 MiB of HBM per device.

v0:
```python
import jax
import jax.numpy as jnp
from jax import lax
from jax.sharding import PartitionSpec as P

eps_norm = 1e-05


def passed_along(block, axis, distance):
    devices = range(lax.axis_size(axis))
    route = [(i - distance, i) for i in devices if i - distance in devices]
    return lax.ppermute(block, axis, route)


def collect_rows(values):
    return lax.all_gather(values, "mp", axis=1, tiled=True)


def sum_features(values):
    return lax.psum_scatter(values, "mp", scatter_dimension=1, tiled=True)


def total_row_count(values):
    return lax.psum(values, "mp")


def body(
    tokens,
    in_weight,
    conv_kernel,
    out_weight,
    gate_weight,
    up_weight,
    down_weight,
    mixer_norm_gain,
    gain_ffn,
    cotangent,
):
    f32 = jnp.float32
    brain_float_sixteen = jnp.bfloat16
    feature_width = tokens.shape[1]
    hidden_model_width = feature_width * lax.axis_size("mp")
    start_position = lax.axis_index("mp") * feature_width
    mix_slice = lax.dynamic_slice_in_dim(mixer_norm_gain, start_position, feature_width)
    feedforward_portion = lax.dynamic_slice_in_dim(gain_ffn, start_position, feature_width)
    w_in, w_out, w_gate, w_up, w_down = (
        lax.all_gather(in_weight, ("dp", "tok"), axis=0, tiled=True),
        lax.all_gather(out_weight, ("dp", "tok"), axis=1, tiled=True),
        lax.all_gather(gate_weight, ("dp", "tok"), axis=0, tiled=True),
        lax.all_gather(up_weight, ("dp", "tok"), axis=0, tiled=True),
        lax.all_gather(down_weight, ("dp", "tok"), axis=1, tiled=True),
    )
    taps = conv_kernel.astype(f32)
    complete_inputs = collect_rows(tokens).astype(f32)
    mixer_inverse_norm = lax.rsqrt(
        jnp.mean(complete_inputs * complete_inputs, -1, keepdims=True) + eps_norm
    )
    complete_normalized = complete_inputs * mixer_inverse_norm
    mixer_hidden = (complete_normalized * mixer_norm_gain).astype(brain_float_sixteen)
    proj = jnp.einsum("td,dkc->tkc", mixer_hidden, w_in, preferred_element_type=f32)
    gate_b = proj[:, 0]
    gate_c = proj[:, 1]
    gate_x = proj[:, 2]
    gated = (gate_b * gate_x).astype(brain_float_sixteen)
    edge = passed_along(gated[-2:], "tok", 1)
    extended = jnp.concatenate([edge, gated], 0).astype(f32)
    rows_count = gated.shape[0]
    conv = (
        taps[0] * extended[0:rows_count]
        + taps[1] * extended[1 : rows_count + 1]
        + taps[2] * extended[2:]
    )
    mixed_in = (gate_c * conv).astype(brain_float_sixteen)
    residual_stream = tokens.astype(f32) + sum_features(
        jnp.dot(mixed_in, w_out, preferred_element_type=f32)
    )
    square_sum = total_row_count(jnp.sum(residual_stream * residual_stream, -1))
    feedforward_inverse_norm = lax.rsqrt(square_sum[:, None] / hidden_model_width + eps_norm)
    feedforward_normalized = residual_stream * feedforward_inverse_norm
    feedforward_hidden = collect_rows(
        (feedforward_normalized * feedforward_portion).astype(brain_float_sixteen)
    )
    gate = jnp.dot(feedforward_hidden, w_gate, preferred_element_type=f32)
    upper = jnp.dot(feedforward_hidden, w_up, preferred_element_type=f32)
    sigma = jax.nn.sigmoid(gate)
    silu_gate = gate * sigma
    hidden = (silu_gate * upper).astype(brain_float_sixteen)
    result = residual_stream + sum_features(jnp.dot(hidden, w_down, preferred_element_type=f32))
    mixed = result.astype(brain_float_sixteen)
    cot_full = collect_rows(cotangent)
    dhidden = jnp.einsum("td,fd->tf", cot_full, w_down, preferred_element_type=f32)
    grad_down = jnp.einsum("tf,td->fd", hidden, cot_full, preferred_element_type=f32)
    dgate = (dhidden * upper * sigma * (1.0 + gate * (1.0 - sigma))).astype(brain_float_sixteen)
    dupper = (dhidden * silu_gate).astype(brain_float_sixteen)
    grad_gate = jnp.einsum("td,tf->df", feedforward_hidden, dgate, preferred_element_type=f32)
    grad_up = jnp.einsum("td,tf->df", feedforward_hidden, dupper, preferred_element_type=f32)
    back_ffn = jnp.einsum("tf,df->td", dgate, w_gate, preferred_element_type=f32) + jnp.einsum(
        "tf,df->td", dupper, w_up, preferred_element_type=f32
    )
    feedforward_hidden_gradient = sum_features(back_ffn)
    feedforward_gain_gradient = jnp.sum(feedforward_hidden_gradient * feedforward_normalized, 0)
    feedforward_scaled_input = feedforward_hidden_gradient * feedforward_portion
    feedforward_dot_product = total_row_count(
        jnp.sum(feedforward_scaled_input * feedforward_normalized, -1)
    )
    residual_gradient = cotangent.astype(f32) + feedforward_inverse_norm * (
        feedforward_scaled_input
        - feedforward_normalized * (feedforward_dot_product[:, None] / hidden_model_width)
    )
    dresid_full = collect_rows(residual_gradient.astype(brain_float_sixteen))
    grad_out = jnp.einsum("tc,td->cd", mixed_in, dresid_full, preferred_element_type=f32)
    dmixed = jnp.einsum("td,cd->tc", dresid_full, w_out, preferred_element_type=f32)
    dconv = (dmixed * gate_c).astype(brain_float_sixteen)
    dgate_c = dmixed * conv
    after = passed_along(dconv[:2], "tok", -1)
    dconv_ext = jnp.concatenate([dconv, after], 0).astype(f32)
    dconv_own = dconv_ext[0:rows_count]
    grad_taps = jnp.stack(
        [
            jnp.sum(dconv_own * extended[0:rows_count], 0),
            jnp.sum(dconv_own * extended[1 : rows_count + 1], 0),
            jnp.sum(dconv_own * extended[2:], 0),
        ],
        0,
    )
    dgated = taps[2] * dconv_own + taps[1] * dconv_ext[1 : rows_count + 1] + taps[0] * dconv_ext[2:]
    dproj = jnp.stack([dgated * gate_x, dgate_c, dgated * gate_b], 1).astype(brain_float_sixteen)
    grad_in = jnp.einsum("td,tkc->dkc", mixer_hidden, dproj, preferred_element_type=f32)
    mixer_hidden_gradient = sum_features(
        jnp.einsum("tkc,dkc->td", dproj, w_in, preferred_element_type=f32)
    )
    mixer_normalized = lax.dynamic_slice_in_dim(
        complete_normalized, start_position, feature_width, 1
    )
    mixer_gain_gradient = jnp.sum(mixer_hidden_gradient * mixer_normalized, 0)
    mixer_scaled_input = mixer_hidden_gradient * mix_slice
    mixer_dot_product = total_row_count(jnp.sum(mixer_scaled_input * mixer_normalized, -1))
    input_token_gradient = residual_gradient + mixer_inverse_norm * (
        mixer_scaled_input - mixer_normalized * (mixer_dot_product[:, None] / hidden_model_width)
    )
    grad_taps, mixer_gain_gradient, feedforward_gain_gradient = lax.psum(
        (grad_taps, mixer_gain_gradient, feedforward_gain_gradient), ("dp", "tok")
    )
    g_in, g_out, g_gate, g_up, g_down = (
        lax.psum_scatter(grad_in, ("dp", "tok"), scatter_dimension=0, tiled=True),
        lax.psum_scatter(grad_out, ("dp", "tok"), scatter_dimension=1, tiled=True),
        lax.psum_scatter(grad_gate, ("dp", "tok"), scatter_dimension=0, tiled=True),
        lax.psum_scatter(grad_up, ("dp", "tok"), scatter_dimension=0, tiled=True),
        lax.psum_scatter(grad_down, ("dp", "tok"), scatter_dimension=1, tiled=True),
    )
    return (
        mixed,
        input_token_gradient,
        g_in,
        grad_taps,
        g_out,
        g_gate,
        g_up,
        g_down,
        mixer_gain_gradient,
        feedforward_gain_gradient,
    )


def solution(mesh):
    return jax.shard_map(
        body,
        mesh=mesh,
        in_specs=(
            P(("dp", "tok"), "mp"),
            P(("dp", "tok"), None, "mp"),
            P(None, "mp"),
            P("mp", ("dp", "tok")),
            P(("dp", "tok"), "mp"),
            P(("dp", "tok"), "mp"),
            P("mp", ("dp", "tok")),
            P(),
            P(),
            P(("dp", "tok"), "mp"),
        ),
        out_specs=(
            P(("dp", "tok"), "mp"),
            P(("dp", "tok"), "mp"),
            P(("dp", "tok"), None, "mp"),
            P(None, "mp"),
            P("mp", ("dp", "tok")),
            P(("dp", "tok"), "mp"),
            P(("dp", "tok"), "mp"),
            P("mp", ("dp", "tok")),
            P("mp"),
            P("mp"),
        ),
        check_vma=False,
    )
```

profile of v0, /device:TPU:0, one launch (start us, length us, event | category | flops | bytes accessed | tf_op | source)
XLA Modules:
  0.0 1189.8 jit_solution(4125879485622382611)
XLA Ops:
  8.7 30.9 %all_gather.29 = bf16[256,1024]{1,0:T(8,128)(2,1)S(1)} all-gather(bf16[256,128]{1,0:T(8,128)(2,1)} %param.13), channel_id=1, replica_groups=mesh['dp'=2,'tok'=4,'mp'=4] {'dp','tok'}, dimensions={1}, use_global_device_ids=true | all-gather | bytes 589824 | tf_op jit(solution)/shard_map/all_gather | solution.py:48
  50.4 43.3 %all-gather.11.cloned.1.call-done = bf16[1024,3,256]{2,0,1:T(8,128)(2,1)} async-done(((bf16[128,3,256]{2,0,1:T(8,128)(2,1)}), bf16[1024,3,256]{2,0,1:T(8,128)(2,1)}) %all-gather.11.cloned.1.call-update) | async-done | bytes 1572880 | tf_op jit(solution)/shard_map/all_gather | solution.py:47
  114.0 69.7 %reduce-scatter.10.cloned.1.call-done = f32[2048,256]{1,0:T(8,128)} async-done(((f32[2048,1024]{1,0:T(8,128)}), f32[2048,256]{1,0:T(8,128)}) %reduce-scatter.10.cloned.1.call-update) | async-done | bytes 2097168 | tf_op jit(solution)/shard_map/reduce_scatter | solution.py:20
  198.2 39.8 %all-gather.15.cloned.1.call-done = bf16[1024,1152]{1,0:T(8,128)(2,1)} async-done(((bf16[128,1152]{1,0:T(8,128)(2,1)}), bf16[1024,1152]{1,0:T(8,128)(2,1)}) %all-gather.15.cloned.1.call-update) | async-done | bytes 2359312 | tf_op jit(solution)/shard_map/all_gather | solution.py:49
  238.0 35.7 %all-gather.13.cloned.1.call-done = bf16[2048,1024]{1,0:T(8,128)(2,1)} async-done(((bf16[2048,256]{1,0:T(8,128)(2,1)}), bf16[2048,1024]{1,0:T(8,128)(2,1)}) %all-gather.13.cloned.1.call-update) | async-done | bytes 4194320 | tf_op jit(solution)/shard_map/all_gather | solution.py:16
  273.6 10.2 fusion.18
  283.8 44.0 %all-gather.17.cloned.1.call-done = bf16[1024,1152]{1,0:T(8,128)(2,1)} async-done(((bf16[128,1152]{1,0:T(8,128)(2,1)}), bf16[1024,1152]{1,0:T(8,128)(2,1)}) %all-gather.17.cloned.1.call-update) | async-done | bytes 2359312 | tf_op jit(solution)/shard_map/all_gather | solution.py:50
  327.9 10.2 fusion.19
  338.1 44.3 %all-gather.19.cloned.1.call-done = bf16[1152,1024]{1,0:T(8,128)(2,1)} async-done(((bf16[1152,128]{1,0:T(8,128)(2,1)}), bf16[1152,1024]{1,0:T(8,128)(2,1)}) %all-gather.19.cloned.1.call-update) | async-done | bytes 2359312 | tf_op jit(solution)/shard_map/all_gather | solution.py:51
  382.4 34.9 %all-gather.21.cloned.1.call-done = bf16[2048,1024]{1,0:T(8,128)(2,1)} async-done(((bf16[2048,256]{1,0:T(8,128)(2,1)}), bf16[2048,1024]{1,0:T(8,128)(2,1)}) %all-gather.21.cloned.1.call-update) | async-done | bytes 4194320 | tf_op jit(solution)/shard_map/all_gather | solution.py:16
  417.3 17.9 %multiply_convert_fusion = (bf16[2048,1152]{1,0:T(8,128)(2,1)}, bf16[2048,1152]{1,0:T(8,128)(2,1)}, bf16[2048,1152]{1,0:T(8,128)(2,1)}) fusion(f32[2048,1152]{1,0:T(8,128)} %fusion.18, f32[2048,1152]{1,0:T(8,128)} %fusion.19, bf16[2048,1024]{1,0:T(8,128)(2,1)} %all-gather.21.cloned.1.call-done, bf16[1152,1024]{1,0:T(8,128)(2,1)} %all-gather.19.cloned.1.call-done), kind=kOutput, calls=%fused_computation.2 | convolution fusion | flops 4867227648 | bytes 39583744 | tf_op jit(solution)/shard_map/td,fd->tf/dot_general | solution.py:91
  451.8 71.8 %reduce-scatter.14.cloned.1.call-done = f32[2048,256]{1,0:T(8,128)} async-done(((f32[2048,1024]{1,0:T(8,128)}), f32[2048,256]{1,0:T(8,128)}) %reduce-scatter.14.cloned.1.call-update) | async-done | bytes 2097168 | tf_op jit(solution)/shard_map/reduce_scatter | solution.py:20
  536.0 36.2 %all-gather.23.cloned.1.call-done = bf16[2048,1024]{1,0:T(8,128)(2,1)} async-done(((bf16[2048,256]{1,0:T(8,128)(2,1)}), bf16[2048,1024]{1,0:T(8,128)(2,1)}) %all-gather.23.cloned.1.call-update) | async-done | bytes 4194320 | tf_op jit(solution)/shard_map/all_gather | solution.py:16
  593.4 10.6 fusion.20
  604.1 11.5 fusion.24
  615.7 10.6 fusion.25
  626.4 9.8 fusion.26
  667.0 22.4 %all-reduce = (f32[3,256]{1,0:T(4,128)}, f32[256]{0:T(256)}, f32[256]{0:T(256)}) all-reduce(f32[3,256]{1,0:T(4,128)S(1)} %pad_maximum_fusion.3, f32[256]{0:T(256)S(1)} %get-tuple-element.10, f32[256]{0:T(256)S(1)} %get-tuple-element.15), channel_id=1, replica_groups=mesh['dp'=2,'tok'=4,'mp'=4] {'dp','tok'}, use_global_device_ids=true, to_apply=%region_15.0 | all-reduce | flops 1280 | bytes 10240 | tf_op jit(solution)/shard_map/psum | solution.py:141
  695.7 43.2 %reduce-scatter.12.cloned.1.call-done = f32[2048,256]{1,0:T(8,128)} async-done(((f32[2048,1024]{1,0:T(8,128)}), f32[2048,256]{1,0:T(8,128)}) %reduce-scatter.12.cloned.1.call-update) | async-done | bytes 2097168 | tf_op jit(solution)/shard_map/reduce_scatter | solution.py:20
  744.1 94.0 %reduce-scatter.22.cloned.1.call-done = f32[128,1152]{1,0:T(8,128)} async-done(((f32[1024,1152]{1,0:T(8,128)}), f32[128,1152]{1,0:T(8,128)}) %reduce-scatter.22.cloned.1.call-update) | async-done | bytes 589840 | tf_op jit(solution)/shard_map/reduce_scatter | solution.py:147
  838.1 99.3 %reduce-scatter.24.cloned.1.call-done = f32[128,1152]{1,0:T(8,128)} async-done(((f32[1024,1152]{1,0:T(8,128)}), f32[128,1152]{1,0:T(8,128)}) %reduce-scatter.24.cloned.1.call-update) | async-done | bytes 589840 | tf_op jit(solution)/shard_map/reduce_scatter | solution.py:148
  937.4 99.6 %reduce-scatter.26.cloned.1.call-done = f32[1152,128]{1,0:T(8,128)} async-done(((f32[1152,1024]{1,0:T(8,128)}), f32[1152,128]{1,0:T(8,128)}) %reduce-scatter.26.cloned.1.call-update) | async-done | bytes 589840 | tf_op jit(solution)/shard_map/reduce_scatter | solution.py:149
  1036.9 67.6 %reduce-scatter.20.cloned.1.call-done = f32[256,128]{1,0:T(8,128)} async-done(((f32[256,1024]{1,0:T(8,128)}), f32[256,128]{1,0:T(8,128)}) %reduce-scatter.20.cloned.1.call-update) | async-done | bytes 131088 | tf_op jit(solution)/shard_map/reduce_scatter | solution.py:146
  1104.6 78.4 %reduce-scatter.18.cloned.1.call-done = f32[128,3,256]{2,0,1:T(8,128)} async-done(((f32[1024,3,256]{2,0,1:T(8,128)}), f32[128,3,256]{2,0,1:T(8,128)}) %reduce-scatter.18.cloned.1.call-update) | async-done | bytes 393232 | tf_op jit(solution)/shard_map/reduce_scatter | solution.py:145
  (113 shorter events, 139.3 us)
Async XLA Ops:
  7.2 40.1 %all-gather.9.cloned.1.call-start = ((), (), s32[]{:S(2)}) async-start(), calls=%async_computation.9 | async-start | bytes 5242880 | tf_op jit(solution)/shard_map/all_gather | solution.py:16
  7.9 85.8 %all-gather.11.cloned.1.call-start = ((), (), s32[]{:S(2)}) async-start(), calls=%async_computation.10 | async-start | bytes 1769472 | tf_op jit(solution)/shard_map/all_gather | solution.py:47
  8.7 85.0 %copy-start.11 = (f32[1024]{0:T(1024)S(1)}, f32[1024]{0:T(1024)}, u32[]{:S(2)}) copy-start(f32[1024]{0:T(1024)} %param.17) | copy-start | bytes 12292
  8.7 175.0 %reduce-scatter.10.cloned.1.call-start = ((), (), s32[]{:S(2)}) async-start(), calls=%async_computation.11 | async-start | bytes 10485760 | tf_op jit(solution)/shard_map/reduce_scatter | solution.py:20
  39.6 67.5 %copy-start.7 = (bf16[256,1024]{1,0:T(8,128)(2,1)}, bf16[256,1024]{1,0:T(8,128)(2,1)S(1)}, u32[]{:S(2)}) copy-start(bf16[256,1024]{1,0:T(8,128)(2,1)S(1)} %all_gather.29) | copy-start | bytes 1572868
  99.7 5.1 collective-permute-start
  112.6 71.1 %copy-start.6 = (bf16[2048,256]{1,0:T(8,128)(2,1)S(1)}, bf16[2048,256]{1,0:T(8,128)(2,1)}, u32[]{:S(2)}) copy-start(bf16[2048,256]{1,0:T(8,128)(2,1)} %param.10) | copy-start | bytes 3145732
  112.6 125.4 %all-gather.15.cloned.1.call-start = ((), (), s32[]{:S(2)}) async-start(), calls=%async_computation.13 | async-start | bytes 2654208 | tf_op jit(solution)/shard_map/all_gather | solution.py:49
  113.2 160.4 %all-gather.13.cloned.1.call-start = ((), (), s32[]{:S(2)}) async-start(), calls=%async_computation.12 | async-start | bytes 5242880 | tf_op jit(solution)/shard_map/all_gather | solution.py:16
  195.8 132.1 %all-gather.17.cloned.1.call-start = ((), (), s32[]{:S(2)}) async-start(), calls=%async_computation.14 | async-start | bytes 2654208 | tf_op jit(solution)/shard_map/all_gather | solution.py:50
  196.4 186.1 %all-gather.19.cloned.1.call-start = ((), (), s32[]{:S(2)}) async-start(), calls=%async_computation.15 | async-start | bytes 2654208 | tf_op jit(solution)/shard_map/all_gather | solution.py:51
  197.1 220.2 %all-gather.21.cloned.1.call-start = ((), (), s32[]{:S(2)}) async-start(), calls=%async_computation.17 | async-start | bytes 5242880 | tf_op jit(solution)/shard_map/all_gather | solution.py:16
  197.9 325.8 %reduce-scatter.14.cloned.1.call-start = ((), (), s32[]{:S(2)}) async-start(), calls=%async_computation.18 | async-start | bytes 10485760 | tf_op jit(solution)/shard_map/reduce_scatter | solution.py:20
  451.8 80.7 %copy-start.2 = (bf16[2048,256]{1,0:T(8,128)(2,1)S(1)}, bf16[2048,256]{1,0:T(8,128)(2,1)}, u32[]{:S(2)}) copy-start(bf16[2048,256]{1,0:T(8,128)(2,1)} %param.19) | copy-start | bytes 3145732
  451.8 120.4 %all-gather.23.cloned.1.call-start = ((), (), s32[]{:S(2)}) async-start(), calls=%async_computation.19 | async-start | bytes 5242880 | tf_op jit(solution)/shard_map/all_gather | solution.py:16
  535.9 128.4 %reduce-scatter.16.cloned.1.call-start = ((), (), s32[]{:S(2)}) async-start(), calls=%async_computation.20 | async-start | bytes 10485760 | tf_op jit(solution)/shard_map/reduce_scatter | solution.py:20
  578.4 5.6 collective-permute-start.1
  593.3 145.6 %reduce-scatter.12.cloned.1.call-start = ((), (), s32[]{:S(2)}) async-start(), calls=%async_computation.16 | async-start | bytes 10485760 | tf_op jit(solution)/shard_map/reduce_scatter | solution.py:20
  604.0 234.1 %reduce-scatter.22.cloned.1.call-start = ((), (), s32[]{:S(2)}) async-start(), calls=%async_computation.23 | async-start | bytes 5308416 | tf_op jit(solution)/shard_map/reduce_scatter | solution.py:147
  615.6 321.8 %reduce-scatter.24.cloned.1.call-start = ((), (), s32[]{:S(2)}) async-start(), calls=%async_computation.24 | async-start | bytes 5308416 | tf_op jit(solution)/shard_map/reduce_scatter | solution.py:148
  626.3 410.6 %reduce-scatter.26.cloned.1.call-start = ((), (), s32[]{:S(2)}) async-start(), calls=%async_computation.25 | async-start | bytes 5308416 | tf_op jit(solution)/shard_map/reduce_scatter | solution.py:149
  636.2 468.4 %reduce-scatter.20.cloned.1.call-start = ((), (), s32[]{:S(2)}) async-start(), calls=%async_computation.22 | async-start | bytes 1179648 | tf_op jit(solution)/shard_map/reduce_scatter | solution.py:146
  642.0 541.1 %reduce-scatter.18.cloned.1.call-start = ((), (), s32[]{:S(2)}) async-start(), calls=%async_computation.21 | async-start | bytes 3538944 | tf_op jit(solution)/shard_map/reduce_scatter | solution.py:145
  656.7 82.2 %copy-start = (f32[2048,256]{1,0:T(8,128)S(1)}, f32[2048,256]{1,0:T(8,128)}, u32[]{:S(2)}) copy-start(f32[2048,256]{1,0:T(8,128)} %get-tuple-element.23) | copy-start | bytes 6291460
  (13 other events, 75.9 us)
Sparse Core Ops, SparseCore 0:
  9.6 37.7 all-gather.8
  49.5 44.1 all-gather.10
  112.7 70.8 reduce-scatter.9
  185.8 52.0 all-gather.14
  240.0 33.5 all-gather.12
  275.8 52.0 all-gather.16
  330.1 52.2 all-gather.18
  384.0 33.2 all-gather.20
  451.9 71.6 reduce-scatter.13
  536.0 36.1 all-gather.22
  593.4 70.7 reduce-scatter.15
  666.9 71.9 reduce-scatter.11
  743.1 94.9 reduce-scatter.21
  842.2 95.1 reduce-scatter.23
  941.5 95.4 reduce-scatter.25
  1040.8 63.7 reduce-scatter.19
  1109.1 73.9 reduce-scatter.17
where the time goes:
time: 1200 us; the launch traced here: 1190 us
  waiting for transfers between devices  926 us (77%)
  matrix products  130 us (11%)
  blocking collectives  71.4 us (6%)
  other arithmetic  36.5 us (3%)
  between operations  14.5 us (1%)
    reduce_scatter x4, waiting for transfers between devices, sum_features(): return lax.psum_scatter(values, 'mp', scatter_dimension=1, tiled=True)  192 us
    all_gather x4, waiting for transfers between devices, collect_rows(): return lax.all_gather(values, 'mp', axis=1, tiled=True)  114 us
    reduce_scatter x1, waiting for transfers between devices, body(): lax.psum_scatter(grad_down, ('dp', 'tok'), scatter_dimension=1, tiled=True)  99.6 us
    reduce_scatter x1, waiting for transfers between devices, body(): lax.psum_scatter(grad_up, ('dp', 'tok'), scatter_dimension=0, tiled=True)  99.3 us
    reduce_scatter x1, waiting for transfers between devices, body(): lax.psum_scatter(grad_gate, ('dp', 'tok'), scatter_dimension=0, tiled=True)  94 us
    reduce_scatter x1, waiting for transfers between devices, body(): lax.psum_scatter(grad_in, ('dp', 'tok'), scatter_dimension=0, tiled=True)  78.4 us
    reduce_scatter x1, waiting for transfers between devices, body(): lax.psum_scatter(grad_out, ('dp', 'tok'), scatter_dimension=1, tiled=True)  67.6 us
    all_gather x1, waiting for transfers between devices, body(): lax.all_gather(down_weight, ('dp', 'tok'), axis=1, tiled=True)  44.3 us
  transfers between devices with their start and end apart: 19, of which 19 were waited for; matrix products, arithmetic and copies ran while one was open for 8% of the time, Pallas kernels for 0%

commit v1 on v0

--- a/solution.py
+++ b/solution.py
@@ -6,6 +6,28 @@
 eps_norm = 1e-05
 
 
+def laid_out(pieces, dim):
+    shape = list(pieces.shape[1:])
+    shape[dim] *= pieces.shape[0]
+    return jnp.moveaxis(pieces, 0, dim).reshape(shape)
+
+
+def collected_by_bits(x, axis):
+    devices = lax.axis_size(axis)
+    blocks = x[None]
+    for level in range(devices.bit_length() - 1):
+        distance = 1 << level
+        other = lax.ppermute(blocks, axis, [(i, i ^ distance) for i in range(devices)])
+        both = jnp.stack([blocks, other])
+        upper = lax.axis_index(axis) >> level & 1
+        blocks = jnp.where(upper == 0, both, both[::-1]).reshape(-1, *x.shape)
+    return blocks
+
+
+def collect(x, axis, dim):
+    return laid_out(collected_by_bits(x, axis), dim)
+
+
 def passed_along(block, axis, distance):
     devices = range(lax.axis_size(axis))
     route = [(i - distance, i) for i in devices if i - distance in devices]
@@ -13,7 +35,7 @@
 
 
 def collect_rows(values):
-    return lax.all_gather(values, "mp", axis=1, tiled=True)
+    return collect(values, "mp", 1)
 
 
 def sum_features(values):

time: 1200 us -> 1150 us (0.958)
  waiting for transfers between devices: 926 us -> 802 us
  local copies, waits for them, and re-layouts: 4.43 us -> 40.8 us
  other arithmetic: 36.5 us -> 58.7 us
    ppermute x0 -> x8, waiting for transfers between devices: none -> 145 us  [collected_by_bits(): lax.ppermute(blocks, axis, [(i, i ^ distance) for i in range(devices)])]
    all_gather x4 -> x0, waiting for transfers between devices: 114 us -> none  [collect_rows(): return lax.all_gather(values, 'mp', axis=1, tiled=True)]
    all_gather x1, waiting for transfers between devices: 44 us -> 0.01 us  [body(): lax.all_gather(up_weight, ('dp', 'tok'), axis=0, tiled=True)]
    all_gather x1, waiting for transfers between devices: 43.3 us -> 0.01 us  [body(): lax.all_gather(in_weight, ('dp', 'tok'), axis=0, tiled=True)]
    all_gather x1, waiting for transfers between devices: 39.8 us -> 0.01 us  [body(): lax.all_gather(gate_weight, ('dp', 'tok'), axis=0, tiled=True)]
    reduce_scatter x1, waiting for transfers between devices: 99.3 us -> 64.2 us  [body(): lax.psum_scatter(grad_up, ('dp', 'tok'), scatter_dimension=0, tiled=True)]
    reduce_scatter x4, waiting for transfers between devices: 192 us -> 220 us  [sum_features(): return lax.psum_scatter(values, 'mp', scatter_dimension=1, tiled=True)]
    all_gather x1, waiting for transfers between devices: 44.3 us -> 20.2 us  [body(): lax.all_gather(down_weight, ('dp', 'tok'), axis=1, tiled=True)]
  transfers between devices with their start and end apart: 19 -> 23, of which waited for: 19 -> 18; matrix products, arithmetic and copies ran while one was open for 8% -> 13% of each run, Pallas kernels for 0% -> 0%
where the time goes in v1:
time: 1150 us; the launch traced here: 1140 us
  waiting for transfers between devices  802 us (70%)
  matrix products  140 us (12%)
  blocking collectives  71.8 us (6%)
  other arithmetic  58.7 us (5%)
  local copies, waits for them, and re-layouts  40.8 us (4%)
  between operations  14.8 us (1%)
  starting transfers between devices  11.9 us (1%)
    reduce_scatter x4, waiting for transfers between devices, sum_features(): return lax.psum_scatter(values, 'mp', scatter_dimension=1, tiled=True)  220 us
    ppermute x8, waiting for transfers between devices, collected_by_bits(): lax.ppermute(blocks, axis, [(i, i ^ distance) for i in range(devices)])  145 us
    reduce_scatter x1, waiting for transfers between devices, body(): lax.psum_scatter(grad_down, ('dp', 'tok'), scatter_dimension=1, tiled=True)  99.9 us
    reduce_scatter x1, waiting for transfers between devices, body(): lax.psum_scatter(grad_gate, ('dp', 'tok'), scatter_dimension=0, tiled=True)  99.2 us
    reduce_scatter x1, waiting for transfers between devices, body(): lax.psum_scatter(grad_in, ('dp', 'tok'), scatter_dimension=0, tiled=True)  78.7 us
    reduce_scatter x1, waiting for transfers between devices, body(): lax.psum_scatter(grad_out, ('dp', 'tok'), scatter_dimension=1, tiled=True)  67.7 us
    reduce_scatter x1, waiting for transfers between devices, body(): lax.psum_scatter(grad_up, ('dp', 'tok'), scatter_dimension=0, tiled=True)  64.2 us
    all_gather x1, blocking collectives, body(): lax.all_gather(out_weight, ('dp', 'tok'), axis=1, tiled=True)  30.3 us
  transfers between devices with their start and end apart: 23, of which 18 were waited for; matrix products, arithmetic and copies ran while one was open for 13% of the time, Pallas kernels for 0%

profile of v1, /device:TPU:0, one launch (start us, length us, event | category | flops | bytes accessed | tf_op | source)
XLA Modules:
  0.0 1139.6 jit_solution(1431422176254735634)
XLA Ops:
  16.4 30.3 %all_gather.16 = bf16[256,1024]{1,0:T(8,128)(2,1)S(1)} all-gather(bf16[256,128]{1,0:T(8,128)(2,1)S(1)} %copy-done.13), channel_id=1, replica_groups=mesh['dp'=2,'tok'=4,'mp'=4] {'dp','tok'}, dimensions={1}, use_global_device_ids=true | all-gather | bytes 589824 | tf_op jit(solution)/shard_map/all_gather | solution.py:70
  46.7 15.8 %collective-permute-done.1 = bf16[2,2048,256]{2,1,0:T(8,128)(2,1)} collective-permute-done((bf16[2,2048,256]{2,1,0:T(8,128)(2,1)}, bf16[2,2048,256]{2,1,0:T(8,128)(2,1)}, u32[]{:S(2)}, u32[]{:S(2)}) %collective-permute-start.1) | collective-permute-done | bytes 2097184 | tf_op jit(solution)/shard_map/ppermute | solution.py:20
  65.3 13.5 %copy.24 = f32[4,2048,256]{2,0,1:T(4,128)S(1)} copy(f32[4,2048,256]{2,1,0:T(8,128)S(1)} %bitcast.129) | data formatting | bytes 16777216 | tf_op jit(solution)/shard_map/convert_element_type | solution.py:76
  108.3 71.6 %reduce-scatter.10.cloned.1.call-done = f32[2048,256]{1,0:T(8,128)} async-done(((f32[2048,1024]{1,0:T(8,128)}), f32[2048,256]{1,0:T(8,128)}) %reduce-scatter.10.cloned.1.call-update) | async-done | bytes 2097168 | tf_op jit(solution)/shard_map/reduce_scatter | solution.py:42
  200.2 44.0 %collective-permute-done.6 = bf16[2,2048,256]{2,1,0:T(8,128)(2,1)} collective-permute-done((bf16[2,2048,256]{2,1,0:T(8,128)(2,1)}, bf16[2,2048,256]{2,1,0:T(8,128)(2,1)}, u32[]{:S(2)}, u32[]{:S(2)}) %collective-permute-start.6) | collective-permute-done | bytes 2097184 | tf_op jit(solution)/shard_map/ppermute | solution.py:20
  256.1 32.6 %collective-permute-done.4 = bf16[2,2048,256]{2,1,0:T(8,128)(2,1)} collective-permute-done((bf16[2,2048,256]{2,1,0:T(8,128)(2,1)}, bf16[2,2048,256]{2,1,0:T(8,128)(2,1)}, u32[]{:S(2)}, u32[]{:S(2)}) %collective-permute-start.4) | collective-permute-done | bytes 2097184 | tf_op jit(solution)/shard_map/ppermute | solution.py:20
  300.7 10.4 fusion.27
  311.0 10.3 fusion.28
  321.3 20.2 %all-gather.11.cloned.1.call-done = bf16[1152,1024]{1,0:T(8,128)(2,1)} async-done(((bf16[1152,128]{1,0:T(8,128)(2,1)}), bf16[1152,1024]{1,0:T(8,128)(2,1)}) %all-gather.11.cloned.1.call-update) | async-done | bytes 2359312 | tf_op jit(solution)/shard_map/all_gather | solution.py:73
  341.5 18.4 %multiply_convert_fusion = (bf16[2048,1152]{1,0:T(8,128)(2,1)}, bf16[2048,1152]{1,0:T(8,128)(2,1)}, bf16[2048,1152]{1,0:T(8,128)(2,1)}) fusion(f32[2048,1152]{1,0:T(8,128)} %fusion.27, f32[2048,1152]{1,0:T(8,128)} %fusion.28, bf16[2048,1024]{0,1:T(8,128)(2,1)} %bitcast.135, bf16[1152,1024]{1,0:T(8,128)(2,1)} %all-gather.11.cloned.1.call-done), kind=kOutput, calls=%fused_computation | convolution fusion | flops 4867227648 | bytes 39583744 | tf_op jit(solution)/shard_map/td,fd->tf/dot_general | solution.py:113
  359.9 16.2 %fusion.30 = f32[2048,1024]{1,0:T(8,128)S(1)} fusion(bf16[2048,1152]{1,0:T(8,128)(2,1)} %get-tuple-element.29, bf16[1024,1152]{1,0:T(8,128)(2,1)S(1)} %copy-done.17), kind=kOutput, calls=%fused_computation.87 | convolution fusion | flops 4831838208 | bytes 15466496 | tf_op jit(solution)/shard_map/tf,df->td/dot_general | solution.py:119
  384.5 10.6 fusion.29
  395.2 59.3 %reduce-scatter.14.cloned.1.call-done = f32[2048,256]{1,0:T(8,128)} async-done(((f32[2048,1024]{1,0:T(8,128)}), f32[2048,256]{1,0:T(8,128)}) %reduce-scatter.14.cloned.1.call-update) | async-done | bytes 2097168 | tf_op jit(solution)/shard_map/reduce_scatter | solution.py:42
  463.4 65.5 %reduce-scatter.12.cloned.1.call-done = f32[2048,256]{1,0:T(8,128)} async-done(((f32[2048,1024]{1,0:T(8,128)}), f32[2048,256]{1,0:T(8,128)}) %reduce-scatter.12.cloned.1.call-update) | async-done | bytes 2097168 | tf_op jit(solution)/shard_map/reduce_scatter | solution.py:42
  538.2 47.3 %collective-permute-done.8 = bf16[2,2048,256]{2,1,0:T(8,128)(2,1)S(1)} collective-permute-done((bf16[2,2048,256]{2,1,0:T(8,128)(2,1)S(1)}, bf16[2,2048,256]{2,1,0:T(8,128)(2,1)S(1)}, u32[]{:S(2)}, u32[]{:S(2)}) %collective-permute-start.8) | collective-permute-done | bytes 2097184 | tf_op jit(solution)/shard_map/ppermute | solution.py:20
  626.6 11.6 %fusion.33 = f32[1024,1152]{1,0:T(8,128)} fusion(bf16[2048,1024]{0,1:T(8,128)(2,1)} %bitcast.140, bf16[2048,1152]{1,0:T(8,128)(2,1)} %get-tuple-element.29), kind=kOutput, calls=%fused_computation.90 | convolution fusion | flops 4831838208 | bytes 13631488 | tf_op jit(solution)/shard_map/td,tf->df/dot_general | solution.py:117
  638.3 10.3 fusion.35
  663.6 23.7 %reduce-scatter.16.cloned.1.call-done = f32[2048,256]{1,0:T(8,128)} async-done(((f32[2048,1024]{1,0:T(8,128)}), f32[2048,256]{1,0:T(8,128)}) %reduce-scatter.16.cloned.1.call-update) | async-done | bytes 2097168 | tf_op jit(solution)/shard_map/reduce_scatter | solution.py:42
  690.0 23.2 %all-reduce = (f32[3,256]{1,0:T(4,128)}, f32[256]{0:T(256)}, f32[256]{0:T(256)}) all-reduce(f32[3,256]{1,0:T(4,128)S(1)} %pad_maximum_fusion.11, f32[256]{0:T(256)S(1)} %get-tuple-element.10, f32[256]{0:T(256)S(1)} %get-tuple-element.15), channel_id=1, replica_groups=mesh['dp'=2,'tok'=4,'mp'=4] {'dp','tok'}, use_global_device_ids=true, to_apply=%region_15.16 | all-reduce | flops 1280 | bytes 10240 | tf_op jit(solution)/shard_map/psum | solution.py:163
  723.0 64.2 %reduce-scatter.24.cloned.1.call-done = f32[128,1152]{1,0:T(8,128)} async-done(((f32[1024,1152]{1,0:T(8,128)}), f32[128,1152]{1,0:T(8,128)}) %reduce-scatter.24.cloned.1.call-update) | async-done | bytes 589840 | tf_op jit(solution)/shard_map/reduce_scatter | solution.py:170
  787.2 99.2 %reduce-scatter.22.cloned.1.call-done = f32[128,1152]{1,0:T(8,128)} async-done(((f32[1024,1152]{1,0:T(8,128)}), f32[128,1152]{1,0:T(8,128)}) %reduce-scatter.22.cloned.1.call-update) | async-done | bytes 589840 | tf_op jit(solution)/shard_map/reduce_scatter | solution.py:169
  886.4 99.9 %reduce-scatter.26.cloned.1.call-done = f32[1152,128]{1,0:T(8,128)} async-done(((f32[1152,1024]{1,0:T(8,128)}), f32[1152,128]{1,0:T(8,128)}) %reduce-scatter.26.cloned.1.call-update) | async-done | bytes 589840 | tf_op jit(solution)/shard_map/reduce_scatter | solution.py:171
  986.3 67.7 %reduce-scatter.20.cloned.1.call-done = f32[256,128]{1,0:T(8,128)} async-done(((f32[256,1024]{1,0:T(8,128)}), f32[256,128]{1,0:T(8,128)}) %reduce-scatter.20.cloned.1.call-update) | async-done | bytes 131088 | tf_op jit(solution)/shard_map/reduce_scatter | solution.py:168
  1053.9 78.7 %reduce-scatter.18.cloned.1.call-done = f32[128,3,256]{2,0,1:T(8,128)} async-done(((f32[1024,3,256]{2,0,1:T(8,128)}), f32[128,3,256]{2,0,1:T(8,128)}) %reduce-scatter.18.cloned.1.call-update) | async-done | bytes 393232 | tf_op jit(solution)/shard_map/reduce_scatter | solution.py:167
  (149 shorter events, 180.3 us)
Async XLA Ops:
  7.2 79.5 %all-gather.5.cloned.1.call-start = ((), (), s32[]{:S(2)}) async-start(), calls=%async_computation.9 | async-start | bytes 1769472 | tf_op jit(solution)/shard_map/all_gather | solution.py:69
  7.2 3.0 collective-permute-start
  13.5 49.1 %collective-permute-start.1 = (bf16[2,2048,256]{2,1,0:T(8,128)(2,1)}, bf16[2,2048,256]{2,1,0:T(8,128)(2,1)}, u32[]{:S(2)}, u32[]{:S(2)}) collective-permute-start(bf16[2,2048,256]{2,1,0:T(8,128)(2,1)} %get-tuple-element.45), channel_id=1, source_target_pairs={{0,2},{1,3},{2,0},{3,1},{4,6},{5,7},{6,4},{7,5},{8,10},{9,11},{10,... | collective-permute-start | bytes 6291464 | tf_op jit(solution)/shard_map/ppermute | solution.py:20
  16.4 163.5 %reduce-scatter.10.cloned.1.call-start = ((), (), s32[]{:S(2)}) async-start(), calls=%async_computation.10 | async-start | bytes 10485760 | tf_op jit(solution)/shard_map/reduce_scatter | solution.py:42
  93.3 5.0 collective-permute-start.2
  106.0 73.9 %copy-start.6 = (bf16[2048,256]{1,0:T(8,128)(2,1)S(1)}, bf16[2048,256]{1,0:T(8,128)(2,1)}, u32[]{:S(2)}) copy-start(bf16[2048,256]{1,0:T(8,128)(2,1)} %param.10) | copy-start | bytes 3145732
  106.1 194.6 %all-gather.7.cloned.1.call-start = ((), (), s32[]{:S(2)}) async-start(), calls=%async_computation.11 | async-start | bytes 2654208 | tf_op jit(solution)/shard_map/all_gather | solution.py:71
  106.8 204.2 %all-gather.9.cloned.1.call-start = ((), (), s32[]{:S(2)}) async-start(), calls=%async_computation.12 | async-start | bytes 2654208 | tf_op jit(solution)/shard_map/all_gather | solution.py:72
  107.4 234.1 %all-gather.11.cloned.1.call-start = ((), (), s32[]{:S(2)}) async-start(), calls=%async_computation.13 | async-start | bytes 2654208 | tf_op jit(solution)/shard_map/all_gather | solution.py:73
  107.4 84.1 %collective-permute-start.5 = (bf16[1,2048,256]{2,1,0:T(8,128)(2,1)}, bf16[1,2048,256]{2,1,0:T(8,128)(2,1)}, u32[]{:S(2)}, u32[]{:S(2)}) collective-permute-start(bf16[1,2048,256]{2,1,0:T(8,128)(2,1)} %bitcast.145), channel_id=1, source_target_pairs={{0,1},{1,0},{2,3},{3,2},{4,5},{5,4},{6,7},{7,6},{8,9},{9,8},{10,11... | collective-permute-start | bytes 3145736 | tf_op jit(solution)/shard_map/ppermute | solution.py:20
  191.4 5.8 collective-permute-start.3
  195.5 48.7 %collective-permute-start.6 = (bf16[2,2048,256]{2,1,0:T(8,128)(2,1)}, bf16[2,2048,256]{2,1,0:T(8,128)(2,1)}, u32[]{:S(2)}, u32[]{:S(2)}) collective-permute-start(bf16[2,2048,256]{2,1,0:T(8,128)(2,1)} %get-tuple-element.41), channel_id=1, source_target_pairs={{0,2},{1,3},{2,0},{3,1},{4,6},{5,7},{6,4},{7,5},{8,10},{9,11},{10,... | collective-permute-start | bytes 6291464 | tf_op jit(solution)/shard_map/ppermute | solution.py:20
  199.8 88.9 %collective-permute-start.4 = (bf16[2,2048,256]{2,1,0:T(8,128)(2,1)}, bf16[2,2048,256]{2,1,0:T(8,128)(2,1)}, u32[]{:S(2)}, u32[]{:S(2)}) collective-permute-start(bf16[2,2048,256]{2,1,0:T(8,128)(2,1)} %get-tuple-element.43), channel_id=1, source_target_pairs={{0,2},{1,3},{2,0},{3,1},{4,6},{5,7},{6,4},{7,5},{8,10},{9,11},{10,... | collective-permute-start | bytes 6291464 | tf_op jit(solution)/shard_map/ppermute | solution.py:20
  200.2 254.4 %reduce-scatter.14.cloned.1.call-start = ((), (), s32[]{:S(2)}) async-start(), calls=%async_computation.15 | async-start | bytes 10485760 | tf_op jit(solution)/shard_map/reduce_scatter | solution.py:42
  384.5 144.4 %reduce-scatter.12.cloned.1.call-start = ((), (), s32[]{:S(2)}) async-start(), calls=%async_computation.14 | async-start | bytes 10485760 | tf_op jit(solution)/shard_map/reduce_scatter | solution.py:42
  395.2 292.1 %reduce-scatter.16.cloned.1.call-start = ((), (), s32[]{:S(2)}) async-start(), calls=%async_computation.16 | async-start | bytes 10485760 | tf_op jit(solution)/shard_map/reduce_scatter | solution.py:42
  534.4 2.7 collective-permute-start.7
  537.8 47.7 %collective-permute-start.8 = (bf16[2,2048,256]{2,1,0:T(8,128)(2,1)S(1)}, bf16[2,2048,256]{2,1,0:T(8,128)(2,1)S(1)}, u32[]{:S(2)}, u32[]{:S(2)}) collective-permute-start(bf16[2,2048,256]{2,1,0:T(8,128)(2,1)S(1)} %get-tuple-element.38), channel_id=1, source_target_pairs={{0,2},{1,3},{2,0},{3,1},{4,6},{5,7},{6,4},{7,5},{8,10},{9,11},{10,... | collective-permute-start | bytes 6291464 | tf_op jit(solution)/shard_map/ppermute | solution.py:20
  601.2 5.6 collective-permute-start.9
  616.3 170.8 %reduce-scatter.24.cloned.1.call-start = ((), (), s32[]{:S(2)}) async-start(), calls=%async_computation.20 | async-start | bytes 5308416 | tf_op jit(solution)/shard_map/reduce_scatter | solution.py:170
  626.6 259.8 %reduce-scatter.22.cloned.1.call-start = ((), (), s32[]{:S(2)}) async-start(), calls=%async_computation.19 | async-start | bytes 5308416 | tf_op jit(solution)/shard_map/reduce_scatter | solution.py:169
  638.2 348.1 %reduce-scatter.26.cloned.1.call-start = ((), (), s32[]{:S(2)}) async-start(), calls=%async_computation.21 | async-start | bytes 5308416 | tf_op jit(solution)/shard_map/reduce_scatter | solution.py:171
  648.6 405.4 %reduce-scatter.20.cloned.1.call-start = ((), (), s32[]{:S(2)}) async-start(), calls=%async_computation.18 | async-start | bytes 1179648 | tf_op jit(solution)/shard_map/reduce_scatter | solution.py:168
  654.3 478.4 %reduce-scatter.18.cloned.1.call-start = ((), (), s32[]{:S(2)}) async-start(), calls=%async_computation.17 | async-start | bytes 3538944 | tf_op jit(solution)/shard_map/reduce_scatter | solution.py:167
  (22 other events, 282.2 us)
Sparse Core Ops, SparseCore 0:
  16.5 46.2 all-gather.4
  106.2 73.6 reduce-scatter.9
  182.2 52.0 all-gather.6
  236.5 50.6 all-gather.8
  289.1 52.2 all-gather.10
  384.6 69.9 reduce-scatter.13
  457.1 71.7 reduce-scatter.11
  616.5 70.7 reduce-scatter.15
  691.5 95.6 reduce-scatter.23
  791.2 95.1 reduce-scatter.21
  890.6 95.5 reduce-scatter.25
  990.1 63.7 reduce-scatter.19
  1058.6 74.0 reduce-scatter.17
